TPU v7x, 256 devices: a whole 4x4x8 slice. The times are simulated.
256 devices in a mesh: seq: 64 (over x, z, core), tp: 4 (over y).
Axes of the slice: x: 4, y: 4, z: 8, core: 2. Of those that a mesh axis runs over, the one named last changes fastest.
Arguments:
- hidden_states: bfloat16 [16384, 3584], P('seq', 'tp'), may hold values from -6 to 6
- queries: bfloat16 [16384, 3584], P('seq', 'tp'), may hold values from -6 to 6
- key_weight: bfloat16 [3584, 512], P(None, 'tp'), may hold values from -0.09375 to 0.09375
- value_weight: bfloat16 [3584, 512], P(None, 'tp'), may hold values from -0.09375 to 0.09375
- output_weight: bfloat16 [3584, 3584], P('tp'), may hold values from -1.5 to 1.5
- prefix_keys: bfloat16 [16384, 512], P('seq', 'tp'), may hold values from -64 to 64
- prefix_values: bfloat16 [16384, 512], P('seq', 'tp'), may hold values from -6 to 6
- reads: int32 [64, 16], replicated, may hold values from 0 to 255, as said below
- out_grad: bfloat16 [16384, 3584], P('seq', 'tp'), may hold values from -6 to 6
Outputs:
- layer_output: bfloat16 [16384, 3584], P('seq', 'tp')
- prefix_key_grad: float32 [16384, 512], P('seq', 'tp')
- prefix_value_grad: float32 [16384, 512], P('seq', 'tp')
Inputs may be any that keep to these rules, and one draw needn't show every extreme that they name: Entry l of a row is the row's node at depth l of a prefix tree, one of the blocks l * (16) to (l + 1) * 16 - 1; two rows that share a node share all its ancestors, and all rows share the root. Block b is held by index b // 4 of seq; every row names exactly 1 block of each index that it reads from.
All inputs are finite; a program needn't handle non-finite values.
Results may differ from a plain program's by a relative error of at most 0.0095.
Values may be sent and summed in bfloat16 or wider, within the bound.
A program may use at most 128 MiB of HBM per device.

v0:
```python
import jax
import jax.numpy as jnp
from jax import lax
from jax.sharding import PartitionSpec as P

QH = 28
KVH = 4
HD = 128
PBLK = 64


def local(
    hidden_states,
    queries,
    key_weight,
    value_weight,
    output_weight,
    prefix_keys,
    prefix_values,
    reads,
    out_grad,
):
    length = hidden_states.shape[0]
    scaling = HD ** (-0.5)
    groups = QH // KVH
    cache_cols = key_weight.shape[1]
    seq_count = lax.axis_size("seq")
    own_index = lax.axis_index("seq")
    blocks_here = prefix_keys.shape[0] // PBLK
    flat_width = PBLK * 2 * cache_cols
    read_count = reads.shape[1]
    hidden_piece = lax.all_gather(hidden_states, "tp", axis=1, tiled=True)
    grad_piece = lax.all_gather(out_grad, "tp", axis=1, tiled=True)
    new_keys = jnp.dot(hidden_piece, key_weight, preferred_element_type=jnp.float32)
    new_values = jnp.dot(hidden_piece, value_weight, preferred_element_type=jnp.float32)
    context_grad = lax.dot_general(
        grad_piece, output_weight, (((1,), (1,)), ((), ())), preferred_element_type=jnp.float32
    )
    new_keys = new_keys.astype(jnp.bfloat16)
    new_values = new_values.astype(jnp.bfloat16)
    context_grad = context_grad.astype(jnp.bfloat16)
    my_reads = lax.dynamic_slice_in_dim(reads, own_index, 1, 0)[0]
    local_cache = jnp.concatenate([prefix_keys, prefix_values], axis=1).reshape(
        blocks_here, flat_width
    )
    everything = lax.all_gather(local_cache, "seq", axis=0, tiled=True)
    fetched = jnp.take(everything, my_reads, axis=0)
    fetched_rows = fetched.reshape(read_count * PBLK, 2 * cache_cols)
    causal = jnp.arange(length)[None, :] <= jnp.arange(length)[:, None]
    context_parts = []
    keys_prefix = fetched_rows[:, 0:HD]
    values_prefix = fetched_rows[:, cache_cols : cache_cols + HD]
    key_total = jnp.zeros((read_count * PBLK, HD), jnp.float32)
    value_total = jnp.zeros((read_count * PBLK, HD), jnp.float32)
    for member in range(groups):
        column = member * HD
        head_queries = queries[:, column : column + HD]
        head_grads = context_grad[:, column : column + HD]
        scores_prefix = (
            jnp.einsum("td,pd->tp", head_queries, keys_prefix, preferred_element_type=jnp.float32)
            * scaling
        )
        scores_own = (
            jnp.einsum("td,ud->tu", head_queries, new_keys, preferred_element_type=jnp.float32)
            * scaling
        )
        masked_own = jnp.where(causal, scores_own, -jnp.inf)
        peak_score = jnp.maximum(jnp.max(scores_prefix, axis=-1), jnp.max(masked_own, axis=-1))[
            :, None
        ]
        exps_prefix = jnp.exp(scores_prefix - peak_score)
        exps_own = jnp.exp(masked_own - peak_score)
        denominator = (jnp.sum(exps_prefix, axis=-1) + jnp.sum(exps_own, axis=-1))[:, None]
        softmax_prefix = exps_prefix / denominator
        softmax_own = exps_own / denominator
        weights_prefix = softmax_prefix.astype(jnp.bfloat16)
        weights_own = softmax_own.astype(jnp.bfloat16)
        context = jnp.dot(weights_prefix, values_prefix, preferred_element_type=jnp.float32)
        context = context + jnp.dot(weights_own, new_values, preferred_element_type=jnp.float32)
        context_parts.append(context.astype(jnp.bfloat16))
        slope_prefix = jnp.einsum(
            "td,pd->tp", head_grads, values_prefix, preferred_element_type=jnp.float32
        )
        slope_own = jnp.einsum(
            "td,ud->tu", head_grads, new_values, preferred_element_type=jnp.float32
        )
        row_delta = jnp.sum(softmax_prefix * slope_prefix, axis=-1) + jnp.sum(
            softmax_own * slope_own, axis=-1
        )
        score_grad = (softmax_prefix * (slope_prefix - row_delta[:, None])).astype(jnp.bfloat16)
        value_total = value_total + jnp.einsum(
            "tp,td->pd", weights_prefix, head_grads, preferred_element_type=jnp.float32
        )
        key_total = key_total + jnp.einsum(
            "tp,td->pd", score_grad, head_queries, preferred_element_type=jnp.float32
        )
    key_parts = [key_total * scaling]
    value_parts = [value_total]
    attention = jnp.concatenate(context_parts, axis=1)
    cache_grads = jnp.concatenate(key_parts + value_parts, axis=1).reshape(read_count, flat_width)
    partial_value = jnp.dot(attention, output_weight, preferred_element_type=jnp.float32)
    layer_output = lax.psum_scatter(
        partial_value.astype(jnp.bfloat16), "tp", scatter_dimension=1, tiled=True
    )
    spread = (
        jnp.zeros((seq_count * blocks_here, flat_width), jnp.float32).at[my_reads].set(cache_grads)
    )
    summed = lax.psum_scatter(spread, "seq", scatter_dimension=0, tiled=True)
    summed_rows = summed.reshape(blocks_here * PBLK, 2 * cache_cols)
    return (layer_output, summed_rows[:, :cache_cols], summed_rows[:, cache_cols:])


def solution(mesh):
    in_specs = (
        P("seq", "tp"),
        P("seq", "tp"),
        P(None, "tp"),
        P(None, "tp"),
        P("tp", None),
        P("seq", "tp"),
        P("seq", "tp"),
        P(),
        P("seq", "tp"),
    )
    out_specs = (P("seq", "tp"), P("seq", "tp"), P("seq", "tp"))
    return jax.shard_map(local, mesh=mesh, in_specs=in_specs, out_specs=out_specs, check_vma=False)
```

profile of v0, /device:TPU:1, one launch (start us, length us, event | category | flops | bytes accessed | tf_op | source)
XLA Modules:
  0.0 477.5 jit_solution(8328261768748343851)
XLA Ops:
  11.5 33.5 %all-gather.5.cloned.1.call-done = bf16[256,3584]{1,0:T(8,128)(2,1)} async-done(((bf16[256,896]{1,0:T(8,128)(2,1)}), bf16[256,3584]{1,0:T(8,128)(2,1)}) %all-gather.5.cloned.1.call-update) | async-done | bytes 1835024 | tf_op jit(solution)/shard_map/all_gather | solution.py:32
  45.0 2.1 convolution_convert_fusion.3
  47.1 1.7 fusion.211
  48.8 1.7 fusion.213
  50.6 1.1 fusion.215
  51.6 1.1 fusion.217
  52.7 1.1 fusion.219
  54.2 2.1 convolution_convert_fusion.2
  56.3 21.7 %all-gather.7.cloned.1.call-done = bf16[256,3584]{1,0:T(8,128)(2,1)} async-done(((bf16[256,896]{1,0:T(8,128)(2,1)}), bf16[256,3584]{1,0:T(8,128)(2,1)}) %all-gather.7.cloned.1.call-update) | async-done | bytes 1835024 | tf_op jit(solution)/shard_map/all_gather | solution.py:33
  78.1 6.2 %convolution_convert_fusion.1 = bf16[256,896]{1,0:T(8,128)(2,1)} fusion(bf16[256,3584]{1,0:T(8,128)(2,1)} %all-gather.7.cloned.1.call-done, bf16[896,3584]{1,0:T(8,128)(2,1)} %param.13), kind=kOutput, calls=%fused_computation.12 | convolution fusion | flops 1644396544 | bytes 8716288 | tf_op jit(solution)/shard_map/dot_general | solution.py:36
  84.3 80.6 %all-gather.9.cloned.1.call-done = bf16[64,4,16384]{2,1,0:T(4,128)(2,1)} async-done(((bf16[1,4,16384]{2,1,0:T(4,128)(2,1)}), bf16[64,4,16384]{2,1,0:T(4,128)(2,1)}) %all-gather.9.cloned.1.call-update) | async-done | bytes 8388624 | tf_op jit(solution)/shard_map/all_gather | solution.py:46
  164.9 12.5 %reshape.177 = bf16[256,16384]{1,0:T(8,128)(2,1)} reshape(bf16[64,4,16384]{2,1,0:T(4,128)(2,1)} %all-gather.9.cloned.1.call-done) | data formatting | bytes 16777216
  177.4 5.8 %gather_fusion = bf16[16,16384]{1,0:T(8,128)(2,1)S(1)} fusion(bf16[256,16384]{1,0:T(8,128)(2,1)} %reshape.177, s32[1024]{0:T(1024)S(1)} %pad_clamp_fusion), kind=kCustom, calls=%fused_computation | custom fusion | bytes 1048640 | tf_op jit(solution)/shard_map/jit(_take)/gather | solution.py:47
  186.5 1.2 fusion.81
  187.7 1.4 fusion.50
  190.0 1.3 fusion.48
  192.1 1.3 fusion.46
  194.1 1.4 fusion.44
  196.2 1.3 fusion.42
  198.3 1.3 fusion.40
  200.3 1.3 fusion.38
  204.2 1.0 slice-done
  206.1 2.3 convolution_convert_fusion
  208.4 2.3 copy.63
  210.8 1.8 convolution_add_fusion.5
  213.0 1.7 convolution_add_fusion.4
  215.9 1.6 convolution_add_fusion
  221.5 7.9 %scatter_custom_fusion = f32[256,16384]{1,0:T(8,128)} fusion(s32[16]{0:T(128)S(1)} %fusion.173, f32[16,16384]{1,0:T(8,128)S(1)} %reshape.172, f32[]{:T(128)} %constant.9.clone.1), kind=kCustom, calls=%fused_computation.2 | custom fusion | bytes 16777220 | tf_op jit(solution)/shard_map/scatter | solution.py:106
  231.4 6.6 %reduce-scatter.4.cloned.1.call-done = bf16[896,256]{1,0:T(8,128)(2,1)} async-done(((bf16[3584,256]{1,0:T(8,128)(2,1)}), bf16[896,256]{1,0:T(8,128)(2,1)}) %reduce-scatter.4.cloned.1.call-update) | async-done | bytes 458768
  238.0 2.0 copy.64
  240.0 229.0 %all-reduce.3.cloned.1.call-done = f32[256,16384]{1,0:T(8,128)} async-done(((f32[256,16384]{1,0:T(8,128)}), f32[256,16384]{1,0:T(8,128)}) %all-reduce.3.cloned.1.call-update) | async-done | bytes 16777232
  468.9 1.1 constant_dynamic-slice_fusion
  (165 shorter events, 23.5 us)
Async XLA Ops:
  7.2 37.8 %copy-start = (bf16[3584,128]{1,0:T(8,128)(2,1)S(1)}, bf16[3584,128]{1,0:T(8,128)(2,1)}, u32[]{:S(2)}) copy-start(bf16[3584,128]{1,0:T(8,128)(2,1)} %param.11) | copy-start | bytes 2752516
  7.2 46.6 %copy-start.17 = (bf16[256,896]{1,0:T(8,128)(2,1)S(1)}, bf16[256,896]{1,0:T(8,128)(2,1)}, u32[]{:S(2)}) copy-start(bf16[256,896]{1,0:T(8,128)(2,1)} %param.10) | copy-start | bytes 1376260
  7.2 47.0 %copy-start.16 = (bf16[3584,128]{1,0:T(8,128)(2,1)S(1)}, bf16[3584,128]{1,0:T(8,128)(2,1)}, u32[]{:S(2)}) copy-start(bf16[3584,128]{1,0:T(8,128)(2,1)} %param.12) | copy-start | bytes 2752516
  7.2 37.8 %all-gather.5.cloned.1.call-start = ((), (), s32[]{:S(2)}) async-start(), calls=%async_computation.1 | async-start | bytes 2293760 | tf_op jit(solution)/shard_map/all_gather | solution.py:32
  7.9 70.1 %all-gather.7.cloned.1.call-start = ((), (), s32[]{:S(2)}) async-start(), calls=%async_computation.2 | async-start | bytes 2293760 | tf_op jit(solution)/shard_map/all_gather | solution.py:33
  8.7 156.2 %all-gather.9.cloned.1.call-start = ((), (), s32[]{:S(2)}) async-start(), calls=%async_computation.3 | async-start | bytes 8519680 | tf_op jit(solution)/shard_map/all_gather | solution.py:46
  10.4 227.6 %reduce-scatter.4.cloned.1.call-start = ((), (), s32[]{:S(2)}) async-start(), calls=%async_computation.4 | async-start | bytes 2293760
  183.2 3.2 copy-start.19
  183.5 3.1 copy-start.21
  184.0 17.6 %copy-start.14 = (f32[1024,256]{1,0:T(8,128)}, f32[1024,256]{1,0:T(8,128)S(1)}, u32[]{:S(2)}) copy-start(f32[1024,256]{1,0:T(8,128)S(1)} %get-tuple-element.6) | copy-start | bytes 3145732
  184.4 17.6 %copy-start.12 = (f32[1024,256]{1,0:T(8,128)}, f32[1024,256]{1,0:T(8,128)S(1)}, u32[]{:S(2)}) copy-start(f32[1024,256]{1,0:T(8,128)S(1)} %get-tuple-element.10) | copy-start | bytes 3145732
  184.7 17.6 %copy-start.10 = (f32[1024,256]{1,0:T(8,128)}, f32[1024,256]{1,0:T(8,128)S(1)}, u32[]{:S(2)}) copy-start(f32[1024,256]{1,0:T(8,128)S(1)} %get-tuple-element.14) | copy-start | bytes 3145732
  185.1 17.6 %copy-start.8 = (f32[1024,256]{1,0:T(8,128)}, f32[1024,256]{1,0:T(8,128)S(1)}, u32[]{:S(2)}) copy-start(f32[1024,256]{1,0:T(8,128)S(1)} %get-tuple-element.18) | copy-start | bytes 3145732
  185.5 17.6 %copy-start.6 = (f32[1024,256]{1,0:T(8,128)}, f32[1024,256]{1,0:T(8,128)S(1)}, u32[]{:S(2)}) copy-start(f32[1024,256]{1,0:T(8,128)S(1)} %get-tuple-element.22) | copy-start | bytes 3145732
  185.8 17.7 %copy-start.4 = (f32[1024,256]{1,0:T(8,128)}, f32[1024,256]{1,0:T(8,128)S(1)}, u32[]{:S(2)}) copy-start(f32[1024,256]{1,0:T(8,128)S(1)} %get-tuple-element.26) | copy-start | bytes 3145732
  186.2 17.7 %copy-start.2 = (f32[1024,256]{1,0:T(8,128)}, f32[1024,256]{1,0:T(8,128)S(1)}, u32[]{:S(2)}) copy-start(f32[1024,256]{1,0:T(8,128)S(1)} %get-tuple-element.30) | copy-start | bytes 3145732
  186.4 3.3 copy-start.18
  203.1 2.2 slice-start
  203.5 2.6 slice-start.1
  206.1 4.7 copy-start.22
  210.7 3.9 copy-start.9
  210.8 4.3 copy-start.7
  210.8 258.2 %all-reduce.3.cloned.1.call-start = ((), (), s32[]{:S(2)}) async-start(), calls=%async_computation.5 | async-start | bytes 33554432
  213.0 2.5 copy-start.5
  215.1 2.5 copy-start.15
  215.1 2.5 copy-start.29
  215.5 2.5 copy-start.13
  215.5 2.5 copy-start.23
  215.9 2.5 copy-start.11
  215.9 2.5 copy-start.24
  218.4 1.6 copy-start.27
  229.4 241.5 %copy-start.1 = (bf16[3584,128]{1,0:T(8,128)(2,1)S(1)}, bf16[3584,128]{1,0:T(8,128)(2,1)}, u32[]{:S(2)}) copy-start(bf16[3584,128]{1,0:T(8,128)(2,1)} %param.11) | copy-start | bytes 2752516
  (5 other events, 6.2 us)
Sparse Core Ops, SparseCore 0:
  9.9 35.0 all-gather.4
  46.8 31.2 all-gather.6
  81.4 83.3 all-gather.8
  210.9 27.0 reduce-scatter.3
  241.5 227.3 all-reduce.2
where the time goes:
time: 478 us; the launch traced here: 477 us
  waiting for transfers between devices  373 us (78%)
  matrix products  47.3 us (10%)
  local copies, waits for them, and re-layouts  38.8 us (8%)
  between operations  15.2 us (3%)
    unnamed x7, waiting for transfers between devices  237 us
    all_gather x1, waiting for transfers between devices, local(): everything = lax.all_gather(local_cache, 'seq', axis=0, tiled=True)  80.6 us
    all_gather x1, waiting for transfers between devices, local(): hidden_piece = lax.all_gather(hidden_states, 'tp', axis=1, tiled=True)  33.5 us
    unnamed x70, local copies, waits for them, and re-layouts  22.3 us
    all_gather x1, waiting for transfers between devices, local(): grad_piece = lax.all_gather(out_grad, 'tp', axis=1, tiled=True)  21.7 us
  transfers between devices with their start and end apart: 5, of which 5 were waited for; matrix products, arithmetic and copies ran while one was open for 9% of the time, Pallas kernels for 0%

commit v1 on v0

--- a/solution.py
+++ b/solution.py
@@ -7,6 +7,16 @@
 KVH = 4
 HD = 128
 PBLK = 64
+
+
+def around_the_ring(x, axis, d):
+    size = lax.axis_size(axis)
+    current, blocks = (x, [x])
+    for _ in range(size - 1):
+        current = lax.ppermute(current, axis, [(i, (i + 1) % size) for i in range(size)])
+        blocks.insert(0, current)
+    line = jnp.concatenate(blocks, axis=d)
+    return jnp.roll(line, (lax.axis_index(axis) + 1) * x.shape[d], axis=d)
 
 
 def local(
@@ -30,7 +40,7 @@
     flat_width = PBLK * 2 * cache_cols
     read_count = reads.shape[1]
     hidden_piece = lax.all_gather(hidden_states, "tp", axis=1, tiled=True)
-    grad_piece = lax.all_gather(out_grad, "tp", axis=1, tiled=True)
+    grad_piece = around_the_ring(out_grad, "tp", 1)
     new_keys = jnp.dot(hidden_piece, key_weight, preferred_element_type=jnp.float32)
     new_values = jnp.dot(hidden_piece, value_weight, preferred_element_type=jnp.float32)
     context_grad = lax.dot_general(

time: 478 us -> 457 us (0.956)
  waiting for transfers between devices: 373 us -> 353 us
  matrix products: 47.3 us -> 36.8 us
  starting transfers between devices: 0.2 us -> 6.22 us
    ppermute x0 -> x3, waiting for transfers between devices: none -> 40.9 us  [around_the_ring(): lax.ppermute(current, axis, [(i, (i + 1) % size) for i in range(size)])]
    all_gather x1, waiting for transfers between devices: 33.5 us -> 0.01 us  [local(): hidden_piece = lax.all_gather(hidden_states, 'tp', axis=1, tiled=True)]
    all_gather x1 -> x0, waiting for transfers between devices: 21.7 us -> none  [local(): grad_piece = lax.all_gather(out_grad, 'tp', axis=1, tiled=True)]
    ppermute x0 -> x3, starting transfers between devices: none -> 6.06 us  [around_the_ring(): lax.ppermute(current, axis, [(i, (i + 1) % size) for i in range(size)])]
    unnamed x70 -> x83, local copies, waits for them, and re-layouts: 22.3 us -> 25.1 us
    unnamed x7 -> x6, waiting for transfers between devices: 237 us -> 236 us
  transfers between devices with their start and end apart: 5 -> 7, of which waited for: 5 -> 6; matrix products, arithmetic and copies ran while one was open for 9% -> 7% of each run, Pallas kernels for 0% -> 0%
where the time goes in v1:
time: 457 us; the launch traced here: 456 us
  waiting for transfers between devices  353 us (77%)
  local copies, waits for them, and re-layouts  41.5 us (9%)
  matrix products  36.8 us (8%)
  between operations  15.2 us (3%)
  starting transfers between devices  6.22 us (1%)
    unnamed x6, waiting for transfers between devices  236 us
    all_gather x1, waiting for transfers between devices, local(): everything = lax.all_gather(local_cache, 'seq', axis=0, tiled=True)  76.5 us
    ppermute x3, waiting for transfers between devices, around_the_ring(): lax.ppermute(current, axis, [(i, (i + 1) % size) for i in range(size)])  40.9 us
    unnamed x83, local copies, waits for them, and re-layouts  25.1 us
    dot_general x7, matrix products, local(): jnp.einsum('td,pd->tp', head_grads, values_prefix, preferred_element_type...  9.15 us
  transfers between devices with their start and end apart: 7, of which 6 were waited for; matrix products, arithmetic and copies ran while one was open for 7% of the time, Pallas kernels for 0%

profile of v1, /device:TPU:1, one launch (start us, length us, event | category | flops | bytes accessed | tf_op | source)
XLA Modules:
  0.0 455.9 jit_solution(3391914107465004568)
XLA Ops:
  8.0 0.9 pad_maximum_fusion.1
  9.7 2.2 collective-permute-start
  11.9 9.9 %collective-permute-done = bf16[256,896]{1,0:T(8,128)(2,1)S(1)} collective-permute-done((bf16[256,896]{1,0:T(8,128)(2,1)}, bf16[256,896]{1,0:T(8,128)(2,1)S(1)}, u32[]{:S(2)}, u32[]{:S(2)}) %collective-permute-start) | collective-permute-done | bytes 458784 | tf_op jit(solution)/shard_map/ppermute | solution.py:16
  21.7 1.6 collective-permute-start.1
  24.2 11.7 %collective-permute-done.1 = bf16[256,896]{1,0:T(8,128)(2,1)S(1)} collective-permute-done((bf16[256,896]{1,0:T(8,128)(2,1)S(1)}, bf16[256,896]{1,0:T(8,128)(2,1)S(1)}, u32[]{:S(2)}, u32[]{:S(2)}) %collective-permute-start.1) | collective-permute-done | bytes 458784 | tf_op jit(solution)/shard_map/ppermute | solution.py:16
  35.8 2.3 collective-permute-start.2
  38.4 19.4 %collective-permute-done.2 = bf16[256,896]{1,0:T(8,128)(2,1)S(1)} collective-permute-done((bf16[256,896]{1,0:T(8,128)(2,1)S(1)}, bf16[256,896]{1,0:T(8,128)(2,1)S(1)}, u32[]{:S(2)}, u32[]{:S(2)}) %collective-permute-start.2) | collective-permute-done | bytes 458784 | tf_op jit(solution)/shard_map/ppermute | solution.py:16
  58.4 2.9 fusion.4
  61.3 2.3 convolution_convert_fusion.2
  63.6 0.9 fusion.217
  64.5 0.9 fusion.219
  67.1 76.5 %all-gather.6.cloned.1.call-done = bf16[64,4,16384]{2,1,0:T(4,128)(2,1)} async-done(((bf16[1,4,16384]{2,1,0:T(4,128)(2,1)}), bf16[64,4,16384]{2,1,0:T(4,128)(2,1)}) %all-gather.6.cloned.1.call-update) | async-done | bytes 8388624 | tf_op jit(solution)/shard_map/all_gather | solution.py:56
  143.6 12.5 %reshape.177 = bf16[256,16384]{1,0:T(8,128)(2,1)} reshape(bf16[64,4,16384]{2,1,0:T(4,128)(2,1)} %all-gather.6.cloned.1.call-done) | data formatting | bytes 16777216
  156.1 5.8 %gather_fusion = bf16[16,16384]{1,0:T(8,128)(2,1)S(1)} fusion(bf16[256,16384]{1,0:T(8,128)(2,1)} %reshape.177, s32[1024]{0:T(1024)S(1)} %pad_clamp_fusion), kind=kCustom, calls=%fused_computation | custom fusion | bytes 1048640 | tf_op jit(solution)/shard_map/jit(_take)/gather | solution.py:57
  165.2 1.2 fusion.86
  166.4 1.3 fusion.55
  168.6 1.4 fusion.53
  170.8 1.3 fusion.51
  172.8 1.3 fusion.49
  174.8 1.3 fusion.47
  176.9 1.4 fusion.45
  179.0 1.3 fusion.43
  182.9 1.1 slice-done
  184.8 2.3 convolution_convert_fusion
  187.1 2.3 copy.63
  189.5 1.8 convolution_add_fusion.5
  194.2 1.4 convolution_add_fusion
  200.8 7.9 %scatter_custom_fusion = f32[256,16384]{1,0:T(8,128)} fusion(s32[16]{0:T(128)S(1)} %fusion.178, f32[16,16384]{1,0:T(8,128)S(1)} %reshape.172, f32[]{:T(128)} %constant.55.clone.1), kind=kCustom, calls=%fused_computation.2 | custom fusion | bytes 16777220 | tf_op jit(solution)/shard_map/scatter | solution.py:116
  210.6 6.1 %reduce-scatter.4.cloned.1.call-done = bf16[896,256]{1,0:T(8,128)(2,1)} async-done(((bf16[3584,256]{1,0:T(8,128)(2,1)}), bf16[896,256]{1,0:T(8,128)(2,1)}) %reduce-scatter.4.cloned.1.call-update) | async-done | bytes 458768
  216.7 2.0 copy.64
  218.7 228.7 %all-reduce.3.cloned.1.call-done = f32[256,16384]{1,0:T(8,128)} async-done(((f32[256,16384]{1,0:T(8,128)}), f32[256,16384]{1,0:T(8,128)}) %all-reduce.3.cloned.1.call-update) | async-done | bytes 16777232
  447.4 1.1 constant_dynamic-slice_fusion
  (182 shorter events, 26.2 us)
Async XLA Ops:
  7.2 54.1 %copy-start = (bf16[3584,128]{1,0:T(8,128)(2,1)S(1)}, bf16[3584,128]{1,0:T(8,128)(2,1)}, u32[]{:S(2)}) copy-start(bf16[3584,128]{1,0:T(8,128)(2,1)} %param.11) | copy-start | bytes 2752516
  7.2 50.8 %copy-start.18 = (bf16[256,896]{1,0:T(8,128)(2,1)S(1)}, bf16[256,896]{1,0:T(8,128)(2,1)}, u32[]{:S(2)}) copy-start(bf16[256,896]{1,0:T(8,128)(2,1)} %param.17) | copy-start | bytes 1376260
  7.2 54.1 %all-gather.4.cloned.1.call-start = ((), (), s32[]{:S(2)}) async-start(), calls=%async_computation.1 | async-start | bytes 2293760 | tf_op jit(solution)/shard_map/all_gather | solution.py:42
  7.9 135.6 %all-gather.6.cloned.1.call-start = ((), (), s32[]{:S(2)}) async-start(), calls=%async_computation.2 | async-start | bytes 8519680 | tf_op jit(solution)/shard_map/all_gather | solution.py:56
  9.6 207.0 %reduce-scatter.4.cloned.1.call-start = ((), (), s32[]{:S(2)}) async-start(), calls=%async_computation.3 | async-start | bytes 2293760
  9.7 12.1 %collective-permute-start = (bf16[256,896]{1,0:T(8,128)(2,1)}, bf16[256,896]{1,0:T(8,128)(2,1)S(1)}, u32[]{:S(2)}, u32[]{:S(2)}) collective-permute-start(bf16[256,896]{1,0:T(8,128)(2,1)} %param.17), channel_id=1, source_target_pairs={{0,1},{1,2},{2,3},{3,0},{4,5},{5,6},{6,7},{7,4},{8,9},{9,10},{10,1... | collective-permute-start | bytes 1376264 | tf_op jit(solution)/shard_map/ppermute | solution.py:16
  21.7 14.1 %collective-permute-start.1 = (bf16[256,896]{1,0:T(8,128)(2,1)S(1)}, bf16[256,896]{1,0:T(8,128)(2,1)S(1)}, u32[]{:S(2)}, u32[]{:S(2)}) collective-permute-start(bf16[256,896]{1,0:T(8,128)(2,1)S(1)} %collective-permute-done), channel_id=1, source_target_pairs={{0,1},{1,2},{2,3},{3,0},{4,5},{5,6},{6,7},{7,4},{8,9},{9,10},{10,1... | collective-permute-start | bytes 1376264 | tf_op jit(solution)/shard_map/ppermute | solution.py:16
  35.8 21.9 %collective-permute-start.2 = (bf16[256,896]{1,0:T(8,128)(2,1)S(1)}, bf16[256,896]{1,0:T(8,128)(2,1)S(1)}, u32[]{:S(2)}, u32[]{:S(2)}) collective-permute-start(bf16[256,896]{1,0:T(8,128)(2,1)S(1)} %collective-permute-done.1), channel_id=1, source_target_pairs={{0,1},{1,2},{2,3},{3,0},{4,5},{5,6},{6,7},{7,4},{8,9},{9,10},{10,1... | collective-permute-start | bytes 1376264 | tf_op jit(solution)/shard_map/ppermute | solution.py:16
  38.3 20.0 %copy-start.2 = (bf16[896,3584]{1,0:T(8,128)(2,1)S(1)}, bf16[896,3584]{1,0:T(8,128)(2,1)}, u32[]{:S(2)}) copy-start(bf16[896,3584]{1,0:T(8,128)(2,1)} %param.13) | copy-start | bytes 19267588
  58.4 5.2 %copy-start.20 = (bf16[256,896]{1,0:T(8,128)(2,1)S(1)}, bf16[256,896]{1,0:T(8,128)(2,1)}, u32[]{:S(2)}) copy-start(bf16[256,896]{1,0:T(8,128)(2,1)} %param.10) | copy-start | bytes 1376260
  61.3 5.2 %copy-start.19 = (bf16[3584,128]{1,0:T(8,128)(2,1)S(1)}, bf16[3584,128]{1,0:T(8,128)(2,1)}, u32[]{:S(2)}) copy-start(bf16[3584,128]{1,0:T(8,128)(2,1)} %param.12) | copy-start | bytes 2752516
  61.3 5.2 %copy-start.3 = (bf16[256,3584]{1,0:T(8,128)(2,1)S(1)}, bf16[256,3584]{1,0:T(8,128)(2,1)}, u32[]{:S(2)}) copy-start(bf16[256,3584]{1,0:T(8,128)(2,1)} %all-gather.4.cloned.1.call-done) | copy-start | bytes 5505028
  162.7 17.6 %copy-start.16 = (f32[1024,256]{1,0:T(8,128)}, f32[1024,256]{1,0:T(8,128)S(1)}, u32[]{:S(2)}) copy-start(f32[1024,256]{1,0:T(8,128)S(1)} %get-tuple-element.6) | copy-start | bytes 3145732
  163.0 17.6 %copy-start.14 = (f32[1024,256]{1,0:T(8,128)}, f32[1024,256]{1,0:T(8,128)S(1)}, u32[]{:S(2)}) copy-start(f32[1024,256]{1,0:T(8,128)S(1)} %get-tuple-element.10) | copy-start | bytes 3145732
  163.1 2.1 copy-start.22
  163.4 17.6 %copy-start.12 = (f32[1024,256]{1,0:T(8,128)}, f32[1024,256]{1,0:T(8,128)S(1)}, u32[]{:S(2)}) copy-start(f32[1024,256]{1,0:T(8,128)S(1)} %get-tuple-element.14) | copy-start | bytes 3145732
  163.4 1.8 copy-start.24
  163.8 17.6 %copy-start.10 = (f32[1024,256]{1,0:T(8,128)}, f32[1024,256]{1,0:T(8,128)S(1)}, u32[]{:S(2)}) copy-start(f32[1024,256]{1,0:T(8,128)S(1)} %get-tuple-element.18) | copy-start | bytes 3145732
  164.1 17.6 %copy-start.8 = (f32[1024,256]{1,0:T(8,128)}, f32[1024,256]{1,0:T(8,128)S(1)}, u32[]{:S(2)}) copy-start(f32[1024,256]{1,0:T(8,128)S(1)} %get-tuple-element.22) | copy-start | bytes 3145732
  164.5 17.6 %copy-start.6 = (f32[1024,256]{1,0:T(8,128)}, f32[1024,256]{1,0:T(8,128)S(1)}, u32[]{:S(2)}) copy-start(f32[1024,256]{1,0:T(8,128)S(1)} %get-tuple-element.26) | copy-start | bytes 3145732
  164.9 17.7 %copy-start.4 = (f32[1024,256]{1,0:T(8,128)}, f32[1024,256]{1,0:T(8,128)S(1)}, u32[]{:S(2)}) copy-start(f32[1024,256]{1,0:T(8,128)S(1)} %get-tuple-element.30) | copy-start | bytes 3145732
  166.4 2.0 copy-start.21
  181.8 2.2 slice-start
  182.2 2.6 slice-start.1
  187.1 2.4 copy-start.25
  189.4 2.2 copy-start.13
  189.5 257.9 %all-reduce.3.cloned.1.call-start = ((), (), s32[]{:S(2)}) async-start(), calls=%async_computation.4 | async-start | bytes 33554432
  193.8 1.8 copy-start.17
  193.8 1.8 copy-start.32
  194.2 1.8 copy-start.15
  194.2 1.9 copy-start.26
  208.7 240.7 %copy-start.1 = (bf16[3584,128]{1,0:T(8,128)(2,1)S(1)}, bf16[3584,128]{1,0:T(8,128)(2,1)}, u32[]{:S(2)}) copy-start(bf16[3584,128]{1,0:T(8,128)(2,1)} %param.11) | copy-start | bytes 2752516
  (10 other events, 12.7 us)
Sparse Core Ops, SparseCore 0:
  9.9 46.3 all-gather.3
  59.7 83.8 all-gather.5
  189.6 27.0 reduce-scatter.3
  220.2 227.1 all-reduce.2
